TPU v7x, 256 devices: a whole 4x4x8 slice. The times are simulated.
256 devices in a mesh: cube: 8 (over x, core), blk: 32 (over z, y).
Axes of the slice: x: 4, y: 4, z: 8, core: 2. Of those that a mesh axis runs over, the one named last changes fastest.
Arguments:
- right_side: float32 [4, 8, 32, 32, 64], P(None, 'cube', 'blk'), may hold values from -6 to 6
- diag_inverse: float32 [3840, 32768], P('cube', 'blk'), as said below
- panels: float32 [3, 8, 32, 2, 16, 32], P(None, 'cube', 'blk'), may hold values from -1 to 1
- extend_map: int32 [3, 8, 32, 2, 16], P(None, 'cube', 'blk'), may hold values from 0 to 31
Outputs:
- solution: float32 [4, 8, 32, 32, 64], P(None, 'cube', 'blk')
Inputs may be any that keep to these rules, and one draw needn't show every extreme that they name: `extend_map`: each entry names one of the 32 parent rows held by the receiving device. `diag_inverse`: dense real entries.
All inputs are finite; a program needn't handle non-finite values.
Results may differ from a plain program's by a relative error of at most 0.0001.
Values sent between devices are 32-bit elements; how exact they have to be, the bound alone decides.
A program may use at most 64 MiB of HBM per device.

v0:
```python
import jax
import jax.numpy as jnp
from jax import lax
from jax.sharding import PartitionSpec as P


def from_partner(block, axis, apart):
    count = lax.axis_size(axis)
    route = []
    for low in range(count):
        high = low | 1 << apart
        if high != low and high < count:
            route += [(low, high), (high, low)]
    return lax.ppermute(block, axis, route)


def collect_pairs(residual_rows, tree_level, cube_index):
    gathered = residual_rows
    for bit_index in range(tree_level):
        partner_rows = from_partner(gathered, "cube", bit_index)
        lower_side = cube_index // 2**bit_index % 2 == 0
        gathered = jnp.where(
            lower_side,
            jnp.concatenate([gathered, partner_rows], axis=0),
            jnp.concatenate([partner_rows, gathered], axis=0),
        )
    return gathered


def reduce_pairs(partial_value, tree_level, cube_index):
    for bit_index in reversed(range(tree_level)):
        half_rows = partial_value.shape[0] // 2
        lower_rows = partial_value[:half_rows]
        upper_rows = partial_value[half_rows:]
        lower_side = cube_index // 2**bit_index % 2 == 0
        kept_rows = jnp.where(lower_side, lower_rows, upper_rows)
        sent_rows = jnp.where(lower_side, upper_rows, lower_rows)
        partial_value = kept_rows + from_partner(sent_rows, "cube", bit_index)
    return partial_value


def body(right_side, diag_inverse, panels, extend_map):
    highest = lax.Precision.HIGHEST
    levels = right_side.shape[0]
    local_rows = right_side.shape[3]
    columns_k = right_side.shape[4]
    cube_index = lax.axis_index("cube")
    rhs_rows = right_side[:, 0, 0]
    panel_blocks = panels[:, 0, 0]
    row_maps = extend_map[:, 0, 0]
    row_ids = jnp.arange(local_rows, dtype=jnp.int32)
    update = jnp.zeros((local_rows, columns_k), jnp.float32)
    solved = []
    onehots = []
    diag_blocks = []
    for tree_level in range(levels):
        span_rows = 2**tree_level * local_rows
        offset = (2**tree_level - 1) * local_rows
        diag_block = diag_inverse[offset : offset + span_rows]
        diag_blocks.append(diag_block)
        residual_rows = rhs_rows[tree_level] - update
        column = collect_pairs(residual_rows, tree_level, cube_index)

        def term_rows(first_row, row_count, diag_block=diag_block, column=column):
            return jnp.einsum("ir,ik->rk", diag_block, column, precision=highest)

        solved_rows = lax.psum_scatter(
            term_rows(jnp.int32(0), lax.axis_size("blk") * local_rows),
            "blk",
            scatter_dimension=0,
            tiled=True,
        )
        solved.append(solved_rows)
        if tree_level + 1 < levels:
            onehot = (row_maps[tree_level][..., None] == row_ids).astype(jnp.float32)
            onehots.append(onehot)
            upd_rows = jnp.einsum(
                "hmr,rk->hmk", panel_blocks[tree_level], solved_rows, precision=highest
            )
            extended = jnp.einsum("hmt,hmk->htk", onehot, upd_rows, precision=highest)
            update = extended[0] + from_partner(extended[1], "cube", tree_level)
    results = [None] * levels
    parent = None
    for tree_level in reversed(range(levels)):
        span_rows = 2**tree_level * local_rows
        diag_block = diag_blocks[tree_level]
        work_rows = solved[tree_level]
        if parent is not None:
            partner_rows = from_partner(parent, "cube", tree_level)
            parent_pair = jnp.stack([parent, partner_rows], axis=0)
            fetched = jnp.einsum(
                "hmt,htk->hmk", onehots[tree_level], parent_pair, precision=highest
            )
            work_rows = work_rows - jnp.einsum(
                "hmr,hmk->rk", panel_blocks[tree_level], fetched, precision=highest
            )

        def accumulate(running, shard_rows, first_row, diag_block=diag_block):
            return jnp.einsum("ir,rk->ik", diag_block, shard_rows, precision=highest)

        initial = jnp.zeros((span_rows, columns_k), jnp.float32)
        partial_value = accumulate(
            initial, lax.all_gather(work_rows, "blk", axis=0, tiled=True), jnp.int32(0)
        )
        parent = reduce_pairs(partial_value, tree_level, cube_index)
        results[tree_level] = parent
    return jnp.stack(results)[:, None, None]


def solution(mesh):
    placed = (
        P(None, "cube", "blk", None, None),
        P("cube", "blk"),
        P(None, "cube", "blk", None, None, None),
        P(None, "cube", "blk", None, None),
    )
    return jax.shard_map(
        body,
        mesh=mesh,
        in_specs=placed,
        out_specs=P(None, "cube", "blk", None, None),
        check_vma=False,
    )
```

profile of v0, /device:TPU:4, one launch (start us, length us, event | category | flops | bytes accessed | tf_op | source)
XLA Modules:
  0.0 1131.9 jit_solution(12477692200826738122)
XLA Ops:
  6.5 2.9 fusion.15
  10.2 216.9 %reduce-scatter.11.cloned.1.call-done = f32[32,64]{1,0:T(8,128)} async-done(((f32[1024,64]{1,0:T(8,128)}), f32[32,64]{1,0:T(8,128)}) %reduce-scatter.11.cloned.1.call-update) | async-done | bytes 8208 | tf_op jit(solution)/shard_map/reduce_scatter | solution.py:67
  231.5 1.4 convolution_bitcast_fusion.2
  233.9 211.4 %reduce-scatter.13.cloned.1.call-done = f32[32,64]{1,0:T(8,128)} async-done(((f32[1024,64]{1,0:T(8,128)}), f32[32,64]{1,0:T(8,128)}) %reduce-scatter.13.cloned.1.call-update) | async-done | bytes 8208
  446.5 1.3 collective-permute-start.2
  447.8 2.5 collective-permute-done.2
  451.6 1.2 collective-permute-start.4
  452.8 2.7 collective-permute-done.4
  457.0 211.5 %reduce-scatter.15.cloned.1.call-done = f32[32,64]{1,0:T(8,128)} async-done(((f32[1024,64]{1,0:T(8,128)}), f32[32,64]{1,0:T(8,128)}) %reduce-scatter.15.cloned.1.call-update) | async-done | bytes 8208
  670.3 4.7 collective-permute-done.5
  677.4 2.7 collective-permute-done.7
  680.7 5.2 collective-permute-done.8
  687.8 211.4 %reduce-scatter.17.cloned.1.call-done = f32[32,64]{1,0:T(8,128)} async-done(((f32[1024,64]{1,0:T(8,128)}), f32[32,64]{1,0:T(8,128)}) %reduce-scatter.17.cloned.1.call-update) | async-done | bytes 8208 | tf_op jit(solution)/shard_map/reduce_scatter | solution.py:67
  899.2 48.0 %all_gather.12 = f32[1024,64]{1,0:T(8,128)S(1)} all-gather(f32[32,64]{1,0:T(8,128)} %reduce-scatter.17.cloned.1.call-done), channel_id=1, replica_groups=mesh['cube'=8,'blk'=32] {'blk'}, dimensions={0}, use_global_device_ids=true | all-gather | bytes 270336 | tf_op jit(solution)/shard_map/all_gather | solution.py:103
  948.9 4.9 collective-permute-done.9
  955.0 2.7 collective-permute-done.10
  960.1 4.8 collective-permute-done.12
  965.4 47.6 %all_gather.13 = f32[1024,64]{1,0:T(8,128)S(1)} all-gather(f32[32,64]{1,0:T(8,128)S(1)} %copy.9), channel_id=1, replica_groups=mesh['cube'=8,'blk'=32] {'blk'}, dimensions={0}, use_global_device_ids=true | all-gather | bytes 270336 | tf_op jit(solution)/shard_map/all_gather | solution.py:103
  1014.2 1.2 collective-permute-start.13
  1015.4 2.7 collective-permute-done.13
  1019.6 1.2 collective-permute-start.15
  1020.9 2.6 collective-permute-done.15
  1024.1 48.0 %all_gather.14 = f32[1024,64]{1,0:T(8,128)S(1)} all-gather(f32[32,64]{1,0:T(8,128)S(1)} %copy.10), channel_id=1, replica_groups=mesh['cube'=8,'blk'=32] {'blk'}, dimensions={0}, use_global_device_ids=true | all-gather | bytes 270336 | tf_op jit(solution)/shard_map/all_gather | solution.py:103
  1076.1 47.5 %all_gather.15 = f32[1024,64]{1,0:T(8,128)S(1)} all-gather(f32[32,64]{1,0:T(8,128)S(1)} %fusion.2), channel_id=1, replica_groups=mesh['cube'=8,'blk'=32] {'blk'}, dimensions={0}, use_global_device_ids=true | all-gather | bytes 270336 | tf_op jit(solution)/shard_map/all_gather | solution.py:103
  (91 shorter events, 31.3 us)
Async XLA Ops:
  6.5 443.8 %copy-start.5 = (f32[4,1,1,32,64]{4,3,2,1,0:T(8,128)S(1)}, f32[4,1,1,32,64]{4,3,2,1,0:T(8,128)}, u32[]{:S(2)}) copy-start(f32[4,1,1,32,64]{4,3,2,1,0:T(8,128)} %param.4) | copy-start | bytes 98308
  6.5 449.0 %copy-start = (f32[480,1024]{1,0:T(8,128)S(1)}, f32[480,1024]{1,0:T(8,128)}, u32[]{:S(2)}) copy-start(f32[480,1024]{1,0:T(8,128)} %param.5) | copy-start | bytes 5898244
  6.5 220.6 %reduce-scatter.11.cloned.1.call-start = ((), (), s32[]{:S(2)}) async-start(), calls=%async_computation.4 | async-start | bytes 540672 | tf_op jit(solution)/shard_map/reduce_scatter | solution.py:67
  9.4 435.9 %reduce-scatter.13.cloned.1.call-start = ((), (), s32[]{:S(2)}) async-start(), calls=%async_computation.5 | async-start | bytes 540672
  228.3 1.3 collective-permute-start
  230.3 1.2 collective-permute-start.1
  233.9 434.6 %reduce-scatter.15.cloned.1.call-start = ((), (), s32[]{:S(2)}) async-start(), calls=%async_computation.6 | async-start | bytes 540672
  446.5 3.8 collective-permute-start.2
  450.3 1.3 collective-permute-start.3
  451.6 3.9 collective-permute-start.4
  457.0 442.3 %reduce-scatter.17.cloned.1.call-start = ((), (), s32[]{:S(2)}) async-start(), calls=%async_computation.7 | async-start | bytes 540672 | tf_op jit(solution)/shard_map/reduce_scatter | solution.py:67
  669.7 5.3 collective-permute-start.5
  675.0 1.2 collective-permute-start.6
  676.2 3.9 collective-permute-start.7
  680.1 5.9 collective-permute-start.8
  948.3 5.5 collective-permute-start.9
  953.9 3.9 collective-permute-start.10
  957.9 1.2 collective-permute-start.11
  959.3 5.6 collective-permute-start.12
  1014.2 3.9 collective-permute-start.13
  1018.3 1.2 collective-permute-start.14
  1019.6 3.9 collective-permute-start.15
  1073.1 1.2 collective-permute-start.16
  1074.4 1.2 collective-permute-start.17
  (4 other events, 896.1 us)
Sparse Core Ops, SparseCore 0:
  11.2 215.9 reduce-scatter.10
  234.0 211.2 reduce-scatter.12
  457.1 211.3 reduce-scatter.14
  687.9 211.2 reduce-scatter.16
where the time goes:
time: 1130 us
  waiting for transfers between devices  896 us (79%)
  blocking collectives  191 us (17%)
  matrix products  14.2 us (1%)
  between operations  13.4 us (1%)
    reduce_scatter x2, waiting for transfers between devices, body(): lax.psum_scatter(term_rows(jnp.int32(0), lax.axis_size('blk') * local_row...  428 us
    unnamed x6, waiting for transfers between devices  423 us
    all_gather x4, blocking collectives, body(): lax.all_gather(work_rows, 'blk', axis=0, tiled=True)  191 us
    ppermute x18, waiting for transfers between devices, from_partner(): return lax.ppermute(block, axis, route)  44.9 us
  transfers between devices with their start and end apart: 22, of which 22 were waited for; matrix products, arithmetic and copies ran while one was open for 0% of the time, Pallas kernels for 0%

commit v1 on v0

--- a/solution.py
+++ b/solution.py
@@ -1,7 +1,17 @@
+import functools
 import jax
 import jax.numpy as jnp
 from jax import lax
 from jax.sharding import PartitionSpec as P
+
+
+def hold_knots_over_axis(my_data, a_name):
+    return jnp.concatenate(
+        lax.all_to_all(jnp.stack(lax.axis_size(a_name) * [my_data], axis=0), a_name, 0, 0), axis=0
+    )
+
+
+scan_the_masks = functools.partial(hold_knots_over_axis, a_name="blk")
 
 
 def from_partner(block, axis, apart):
@@ -99,9 +109,7 @@
             return jnp.einsum("ir,rk->ik", diag_block, shard_rows, precision=highest)
 
         initial = jnp.zeros((span_rows, columns_k), jnp.float32)
-        partial_value = accumulate(
-            initial, lax.all_gather(work_rows, "blk", axis=0, tiled=True), jnp.int32(0)
-        )
+        partial_value = accumulate(initial, scan_the_masks(work_rows), jnp.int32(0))
         parent = reduce_pairs(partial_value, tree_level, cube_index)
         results[tree_level] = parent
     return jnp.stack(results)[:, None, None]

time: 1130 us -> 1020 us (0.903)
  blocking collectives: 191 us -> 66.6 us
    reduce_scatter x2 -> x4, waiting for transfers between devices: 428 us -> 851 us  [body(): lax.psum_scatter(term_rows(jnp.int32(0), lax.axis_size('blk') * local_row...]
    unnamed x6 -> x4, waiting for transfers between devices: 423 us -> 0.07 us
    all_gather x4 -> x0, blocking collectives: 191 us -> none  [body(): lax.all_gather(work_rows, 'blk', axis=0, tiled=True)]
    all_to_all x0 -> x4, blocking collectives: none -> 66.6 us  [hold_knots_over_axis(): lax.all_to_all(jnp.stack(lax.axis_size(a_name) * [my_data], axis=0), a_na...]
where the time goes in v1:
time: 1020 us
  waiting for transfers between devices  896 us (88%)
  blocking collectives  66.6 us (7%)
  matrix products  14.1 us (1%)
  between operations  13.5 us (1%)
  starting transfers between devices  10.8 us (1%)
    reduce_scatter x4, waiting for transfers between devices, body(): lax.psum_scatter(term_rows(jnp.int32(0), lax.axis_size('blk') * local_row...  851 us
    all_to_all x4, blocking collectives, hold_knots_over_axis(): lax.all_to_all(jnp.stack(lax.axis_size(a_name) * [my_data], axis=0), a_na...  66.6 us
    ppermute x18, waiting for transfers between devices, from_partner(): return lax.ppermute(block, axis, route)  45 us
  transfers between devices with their start and end apart: 22, of which 22 were waited for; matrix products, arithmetic and copies ran while one was open for 0% of the time, Pallas kernels for 0%

profile of v1, /device:TPU:4, one launch (start us, length us, event | category | flops | bytes accessed | tf_op | source)
XLA Modules:
  0.0 1016.0 jit_solution(13493052934717494582)
XLA Ops:
  6.5 2.9 fusion.15
  10.2 216.9 %reduce-scatter.11.cloned.1.call-done = f32[32,64]{1,0:T(8,128)} async-done(((f32[1024,64]{1,0:T(8,128)}), f32[32,64]{1,0:T(8,128)}) %reduce-scatter.11.cloned.1.call-update) | async-done | bytes 8208 | tf_op jit(solution)/shard_map/reduce_scatter | solution.py:77
  231.5 1.4 convolution_bitcast_fusion.2
  233.9 211.4 %reduce-scatter.13.cloned.1.call-done = f32[32,64]{1,0:T(8,128)} async-done(((f32[1024,64]{1,0:T(8,128)}), f32[32,64]{1,0:T(8,128)}) %reduce-scatter.13.cloned.1.call-update) | async-done | bytes 8208 | tf_op jit(solution)/shard_map/reduce_scatter | solution.py:77
  446.5 1.3 collective-permute-start.2
  447.7 2.5 collective-permute-done.2
  452.8 2.7 collective-permute-done.4
  457.0 211.5 %reduce-scatter.15.cloned.1.call-done = f32[32,64]{1,0:T(8,128)} async-done(((f32[1024,64]{1,0:T(8,128)}), f32[32,64]{1,0:T(8,128)}) %reduce-scatter.15.cloned.1.call-update) | async-done | bytes 8208 | tf_op jit(solution)/shard_map/reduce_scatter | solution.py:77
  670.3 4.7 collective-permute-done.5
  677.4 2.7 collective-permute-done.7
  680.8 5.2 collective-permute-done.8
  687.8 211.5 %reduce-scatter.17.cloned.1.call-done = f32[32,64]{1,0:T(8,128)} async-done(((f32[1024,64]{1,0:T(8,128)}), f32[32,64]{1,0:T(8,128)}) %reduce-scatter.17.cloned.1.call-update) | async-done | bytes 8208 | tf_op jit(solution)/shard_map/reduce_scatter | solution.py:77
  900.4 18.2 %all_to_all.20 = f32[32,1,2048]{2,1,0:T(1,128)S(1)} all-to-all(f32[32,1,2048]{2,1,0:T(1,128)S(1)} %reshape.59), channel_id=1, replica_groups=mesh['cube'=8,'blk'=32] {'blk'}, dimensions={0} | all-to-all | bytes 524288 | tf_op jit(solution)/shard_map/all_to_all | solution.py:10
  922.3 4.9 collective-permute-done.9
  927.3 1.4 collective-permute-start.10
  928.6 2.7 collective-permute-done.10
  933.4 4.9 collective-permute-done.12
  939.1 16.0 %all_to_all.21 = f32[32,1,2048]{2,1,0:T(1,128)S(1)} all-to-all(f32[32,1,2048]{2,1,0:T(1,128)S(1)} %reshape.61), channel_id=1, replica_groups=mesh['cube'=8,'blk'=32] {'blk'}, dimensions={0} | all-to-all | bytes 524288 | tf_op jit(solution)/shard_map/all_to_all | solution.py:10
  958.9 2.7 collective-permute-done.13
  964.3 2.7 collective-permute-done.15
  967.9 15.8 %all_to_all.22 = f32[32,1,2048]{2,1,0:T(1,128)S(1)} all-to-all(f32[32,1,2048]{2,1,0:T(1,128)S(1)} %reshape.63), channel_id=1, replica_groups=mesh['cube'=8,'blk'=32] {'blk'}, dimensions={0} | all-to-all | bytes 524288 | tf_op jit(solution)/shard_map/all_to_all | solution.py:10
  983.7 1.3 reduce.2
  989.6 16.6 %all_to_all.23 = f32[32,1,2048]{2,1,0:T(1,128)S(1)} all-to-all(f32[32,1,2048]{2,1,0:T(1,128)S(1)} %reshape.65), channel_id=1, replica_groups=mesh['cube'=8,'blk'=32] {'blk'}, dimensions={0} | all-to-all | bytes 524288 | tf_op jit(solution)/shard_map/all_to_all | solution.py:10
  1006.3 1.3 reduce.3
  (104 shorter events, 39.4 us)
Async XLA Ops:
  6.5 449.0 %copy-start = (f32[480,1024]{1,0:T(8,128)S(1)}, f32[480,1024]{1,0:T(8,128)}, u32[]{:S(2)}) copy-start(f32[480,1024]{1,0:T(8,128)} %param.5) | copy-start | bytes 5898244
  6.5 443.7 %copy-start.5 = (f32[4,1,1,32,64]{4,3,2,1,0:T(8,128)S(1)}, f32[4,1,1,32,64]{4,3,2,1,0:T(8,128)}, u32[]{:S(2)}) copy-start(f32[4,1,1,32,64]{4,3,2,1,0:T(8,128)} %param.4) | copy-start | bytes 98308
  6.5 220.6 %reduce-scatter.11.cloned.1.call-start = ((), (), s32[]{:S(2)}) async-start(), calls=%async_computation.8 | async-start | bytes 540672 | tf_op jit(solution)/shard_map/reduce_scatter | solution.py:77
  9.4 435.9 %reduce-scatter.13.cloned.1.call-start = ((), (), s32[]{:S(2)}) async-start(), calls=%async_computation.9 | async-start | bytes 540672 | tf_op jit(solution)/shard_map/reduce_scatter | solution.py:77
  228.3 1.3 collective-permute-start
  230.3 1.2 collective-permute-start.1
  233.9 434.6 %reduce-scatter.15.cloned.1.call-start = ((), (), s32[]{:S(2)}) async-start(), calls=%async_computation.10 | async-start | bytes 540672 | tf_op jit(solution)/shard_map/reduce_scatter | solution.py:77
  446.5 3.8 collective-permute-start.2
  450.3 1.3 collective-permute-start.3
  451.6 3.9 collective-permute-start.4
  457.0 442.4 %reduce-scatter.17.cloned.1.call-start = ((), (), s32[]{:S(2)}) async-start(), calls=%async_computation.11 | async-start | bytes 540672 | tf_op jit(solution)/shard_map/reduce_scatter | solution.py:77
  669.7 5.3 collective-permute-start.5
  675.0 1.2 collective-permute-start.6
  676.2 3.9 collective-permute-start.7
  680.1 5.9 collective-permute-start.8
  921.7 5.5 collective-permute-start.9
  927.3 4.1 collective-permute-start.10
  931.5 1.2 collective-permute-start.11
  932.9 5.4 collective-permute-start.12
  957.7 3.9 collective-permute-start.13
  961.8 1.2 collective-permute-start.14
  963.1 3.9 collective-permute-start.15
  986.2 1.2 collective-permute-start.16
  987.6 1.2 collective-permute-start.17
  (4 other events, 508.6 us)
Sparse Core Ops, SparseCore 0:
  11.2 215.9 reduce-scatter.10
  234.0 211.2 reduce-scatter.12
  457.1 211.3 reduce-scatter.14
  687.9 211.3 reduce-scatter.16
